TPU v7x, 32 devices: a whole 2x2x4 slice. The times are simulated.
32 devices in a mesh: tm: 8 (over z, y), head: 4 (over x, core).
Axes of the slice: x: 2, y: 2, z: 4, core: 2. Of those that a mesh axis runs over, the one named last changes fastest.
Arguments:
- queries: bfloat16 [6144, 1536], P('tm', 'head'), may hold values from -6 to 6
- key_rows: bfloat16 [6144, 1536], P('tm', 'head'), may hold values from -6 to 6
- value_rows: bfloat16 [6144, 1536], P('tm', 'head'), may hold values from -6 to 6
- grad_out: bfloat16 [6144, 3072], P('tm', 'head'), may hold values from -192 to 192
- w_out: bfloat16 [1536, 3072], P('head', 'tm'), may hold values from -0.109375 to 0.109375
Outputs:
- grad_queries: bfloat16 [6144, 1536], P('tm', 'head')
- grad_keys: bfloat16 [6144, 1536], P('tm', 'head')
- grad_values: bfloat16 [6144, 1536], P('tm', 'head')
All inputs are finite; a program needn't handle non-finite values.
Results may differ from a plain program's by a relative error of at most 0.0081.
Values may be sent and summed in bfloat16 or wider, within the bound.
No kernel may reach another device: no remote copies, remote signals or barrier semaphores. Data moves between devices by JAX's collectives and lax.ppermute only.
A program may use at most 128 MiB of HBM per device.

v0:
```python
import math
import jax
import jax.numpy as jnp
from jax import lax
from jax.sharding import PartitionSpec as P

HD = 128
TILE_T = 6
TILE_H = 8
TILE_W = 8
VT = 8


def passed_along(block, axis, distance):
    devices = range(lax.axis_size(axis))
    route = [(i - distance, i) for i in devices if i - distance in devices]
    return lax.ppermute(block, axis, route)


def tile_range(index, count):
    return (max(index - 1, 0), min(index + 1, count - 1))


def local(queries, key_rows, value_rows, grad_out, w_out):
    token_count, local_width = queries.shape
    head_count = local_width // HD
    tile_size = TILE_T * TILE_H * TILE_W
    tile_count = token_count // tile_size
    inverse_root = 1.0 / math.sqrt(HD)
    video_place = lax.axis_index("tm") % VT
    flags = (video_place > 0, video_place >= 0, video_place < VT - 1)
    full_grad = lax.all_gather(grad_out, "head", axis=1, tiled=True)
    attn_sum = jnp.einsum(
        "td,hd->th",
        full_grad,
        lax.all_gather(w_out, "tm", axis=1, tiled=True),
        preferred_element_type=jnp.float32,
    )
    attn_grad = attn_sum.astype(jnp.bfloat16)
    before_keys, before_values = passed_along((key_rows, value_rows), "tm", 1)
    after_keys, after_values = passed_along((key_rows, value_rows), "tm", -1)
    slab_keys = (before_keys, key_rows, after_keys)
    slab_values = (before_values, value_rows, after_values)
    zero_tile = jnp.zeros((tile_size, local_width), jnp.float32)
    key_sums = [[zero_tile] * tile_count for other in range(3)]
    value_sums = [[zero_tile] * tile_count for other in range(3)]
    query_grads = []
    for tile_index in range(tile_count):
        lower, upper = tile_range(tile_index, tile_count)
        width_rows = (upper - lower + 1) * tile_size
        key_block = jnp.concatenate([part for part in slab_keys], 0)
        key_block = key_block.reshape(3 * width_rows, head_count, HD)
        value_block = jnp.concatenate([part for part in slab_values], 0)
        value_block = value_block.reshape(3 * width_rows, head_count, HD)
        key_mask = jnp.concatenate([jnp.broadcast_to(flag, (width_rows,)) for flag in flags], 0)
        query_tile = queries[tile_index * tile_size : (tile_index + 1) * tile_size].reshape(
            tile_size, head_count, HD
        )
        grad_tile = attn_grad[tile_index * tile_size : (tile_index + 1) * tile_size].reshape(
            tile_size, head_count, HD
        )
        scores = (
            jnp.einsum("qhd,khd->hqk", query_tile, key_block, preferred_element_type=jnp.float32)
            * inverse_root
        )
        scores = jnp.where(key_mask[None, None, :], scores, -jnp.inf)
        row_peak = jnp.max(scores, axis=2, keepdims=True)
        weights = jnp.exp(scores - row_peak)
        row_total = jnp.sum(weights, axis=2, keepdims=True)
        softmax_rows = weights / row_total
        softmax_grad = jnp.einsum(
            "qhd,khd->hqk", grad_tile, value_block, preferred_element_type=jnp.float32
        )
        row_inner = jnp.sum(softmax_rows * softmax_grad, axis=2, keepdims=True)
        score_grad = (softmax_rows * (softmax_grad - row_inner)).astype(jnp.bfloat16)
        softmax_low = softmax_rows.astype(jnp.bfloat16)
        grad_query = (
            jnp.einsum("hqk,khd->qhd", score_grad, key_block, preferred_element_type=jnp.float32)
            * inverse_root
        )
        query_grads.append(grad_query.reshape(tile_size, local_width).astype(jnp.bfloat16))
        kept = (0, 1, 2)
        key_part = (
            jnp.einsum("hqk,qhd->khd", score_grad, query_tile, preferred_element_type=jnp.float32)
            * inverse_root
        )
        key_part = key_part.reshape(len(kept) * width_rows, local_width)
        value_part = jnp.einsum(
            "hqk,qhd->khd", softmax_low, grad_tile, preferred_element_type=jnp.float32
        )
        value_part = value_part.reshape(len(kept) * width_rows, local_width)
        for position, slab_index in enumerate(kept):
            for neighbour in range(lower, upper + 1):
                offset = position * width_rows + (neighbour - lower) * tile_size
                key_sums[slab_index][neighbour] = (
                    key_sums[slab_index][neighbour] + key_part[offset : offset + tile_size]
                )
                value_sums[slab_index][neighbour] = (
                    value_sums[slab_index][neighbour] + value_part[offset : offset + tile_size]
                )
    own_keys = jnp.concatenate(key_sums[1], 0)
    own_values = jnp.concatenate(value_sums[1], 0)
    later_keys, later_values = (
        passed_along(jnp.concatenate(key_sums[0], 0).astype(jnp.bfloat16), "tm", -1).astype(
            jnp.float32
        ),
        passed_along(jnp.concatenate(value_sums[0], 0).astype(jnp.bfloat16), "tm", -1).astype(
            jnp.float32
        ),
    )
    earlier_keys, earlier_values = (
        passed_along(jnp.concatenate(key_sums[2], 0).astype(jnp.bfloat16), "tm", 1).astype(
            jnp.float32
        ),
        passed_along(jnp.concatenate(value_sums[2], 0).astype(jnp.bfloat16), "tm", 1).astype(
            jnp.float32
        ),
    )
    grad_keys = own_keys + later_keys + earlier_keys
    grad_values = own_values + later_values + earlier_values
    grad_queries = jnp.concatenate(query_grads, 0)
    return (grad_queries, grad_keys.astype(jnp.bfloat16), grad_values.astype(jnp.bfloat16))


def solution(mesh):
    placed = (P("tm", "head"), P("tm", "head"), P("tm", "head"), P("tm", "head"), P("head", "tm"))
    return jax.shard_map(
        local,
        mesh=mesh,
        in_specs=placed,
        out_specs=(P("tm", "head"), P("tm", "head"), P("tm", "head")),
        check_vma=False,
    )
```

profile of v0, /device:TPU:0, one launch (start us, length us, event | category | flops | bytes accessed | tf_op | source)
XLA Modules:
  0.0 249.1 jit_solution(441162464719006397)
XLA Ops:
  7.2 0.7 all-gather.5.cloned.1.call-update
  8.0 0.7 all-gather.3.cloned.1.call-update
  8.7 1.3 copy.44
  10.0 1.3 collective-permute-start.3
  11.3 6.4 %collective-permute-start.2 = (bf16[768,384]{0,1:T(8,128)(2,1)S(1)}, bf16[768,384]{0,1:T(8,128)(2,1)}, u32[]{:S(2)}, u32[]{:S(2)}) collective-permute-start(bf16[768,384]{0,1:T(8,128)(2,1)S(1)} %copy.44), channel_id=1, source_target_pairs={{0,4},{4,8},{8,12},{12,16},{16,20},{20,24},{24,28},{1,5},{5,9},{9,... | collective-permute-start | bytes 1769480 | tf_op jit(solution)/shard_map/ppermute | solution.py:17
  17.6 1.3 copy.38
  18.9 1.3 collective-permute-start.1
  20.2 5.4 %collective-permute-start = (bf16[768,384]{0,1:T(8,128)(2,1)S(1)}, bf16[768,384]{0,1:T(8,128)(2,1)}, u32[]{:S(2)}, u32[]{:S(2)}) collective-permute-start(bf16[768,384]{0,1:T(8,128)(2,1)S(1)} %copy.38), channel_id=1, source_target_pairs={{0,4},{4,8},{8,12},{12,16},{16,20},{20,24},{24,28},{1,5},{5,9},{9,... | collective-permute-start | bytes 1769480 | tf_op jit(solution)/shard_map/ppermute | solution.py:17
  25.8 0.2 copy.94
  26.0 0.2 copy.95
  26.3 5.9 %collective-permute-done.3 = bf16[768,384]{0,1:T(8,128)(2,1)S(1)} collective-permute-done((bf16[768,384]{0,1:T(8,128)(2,1)S(1)}, bf16[768,384]{0,1:T(8,128)(2,1)S(1)}, u32[]{:S(2)}, u32[]{:S(2)}) %collective-permute-start.3) | collective-permute-done | bytes 589856 | tf_op jit(solution)/shard_map/ppermute | solution.py:17
  32.2 24.7 %collective-permute-done.2 = bf16[768,384]{0,1:T(8,128)(2,1)} collective-permute-done((bf16[768,384]{0,1:T(8,128)(2,1)S(1)}, bf16[768,384]{0,1:T(8,128)(2,1)}, u32[]{:S(2)}, u32[]{:S(2)}) %collective-permute-start.2) | collective-permute-done | bytes 589856 | tf_op jit(solution)/shard_map/ppermute | solution.py:17
  56.9 2.5 pad_maximum_fusion.1
  59.4 0.8 copy-done.4
  60.2 11.8 %collective-permute-done = bf16[768,384]{0,1:T(8,128)(2,1)} collective-permute-done((bf16[768,384]{0,1:T(8,128)(2,1)S(1)}, bf16[768,384]{0,1:T(8,128)(2,1)}, u32[]{:S(2)}, u32[]{:S(2)}) %collective-permute-start) | collective-permute-done | bytes 589856 | tf_op jit(solution)/shard_map/ppermute | solution.py:17
  72.0 1.4 pad_maximum_fusion
  73.4 7.7 %fusion.52 = (f32[3,384]{1,0:T(4,128)S(1)}, f32[3,384,2304]{1,2,0:T(8,128)}) fusion(pred[2304]{0:T(1024)(128)(4,1)S(1)} %pad_add_fusion, bf16[2304,3,128]{0,2,1:T(8,128)(2,1)S(1)} %bitcast.78, bf16[384,3,128]{0,2,1:T(8,128)(2,1)S(1)} %bitcast.95), kind=kOutput, calls=%fused_computation.81 | convolution fusion | flops 690096384 | bytes 12688128 | tf_op jit(solution)/shard_map/sub | solution.py:68
  81.0 7.8 %fusion.53 = (f32[3,384]{1,0:T(4,128)S(1)}, f32[3,384,2304]{1,2,0:T(8,128)}) fusion(pred[2304]{0:T(1024)(128)(4,1)S(1)} %pad_add_fusion, bf16[2304,3,128]{0,2,1:T(8,128)(2,1)S(1)} %bitcast.79, bf16[384,3,128]{0,2,1:T(8,128)(2,1)S(1)} %bitcast.92), kind=kOutput, calls=%fused_computation.82 | convolution fusion | flops 690096384 | bytes 12688128 | tf_op jit(solution)/shard_map/sub | solution.py:68
  88.9 3.6 %all-gather.5.cloned.1.call-done = bf16[384,3072]{1,0:T(8,128)(2,1)} async-done(((bf16[384,384]{1,0:T(8,128)(2,1)}), bf16[384,3072]{1,0:T(8,128)(2,1)}) %all-gather.5.cloned.1.call-update) | async-done | bytes 2359312 | tf_op jit(solution)/shard_map/all_gather | solution.py:36
  92.5 39.1 %all-gather.3.cloned.1.call-done = bf16[768,3072]{1,0:T(8,128)(2,1)} async-done(((bf16[768,768]{1,0:T(8,128)(2,1)}), bf16[768,3072]{1,0:T(8,128)(2,1)}) %all-gather.3.cloned.1.call-update) | async-done | bytes 4718608 | tf_op jit(solution)/shard_map/all_gather | solution.py:32
  131.6 5.1 %convolution_convert_fusion = bf16[768,384]{0,1:T(8,128)(2,1)S(1)} fusion(bf16[768,3072]{1,0:T(8,128)(2,1)} %all-gather.3.cloned.1.call-done, bf16[384,3072]{1,0:T(8,128)(2,1)} %all-gather.5.cloned.1.call-done), kind=kOutput, calls=%fused_computation.36 | convolution fusion | flops 1812234240 | bytes 7667712 | tf_op jit(solution)/shard_map/td,hd->th/dot_general | solution.py:33
  136.8 5.8 %fusion.25 = f32[2304,3,128]{0,2,1:T(8,128)S(1)} fusion(bf16[384,3,128]{0,2,1:T(8,128)(2,1)S(1)} %bitcast.108, f32[3,384,2304]{1,2,0:T(8,128)} %get-tuple-element.20, f32[3,384]{1,0:T(4,128)S(1)} %get-tuple-element.19), kind=kOutput, calls=%fused_computation.33 | convolution fusion | flops 684785664 | bytes 14455296 | tf_op jit(solution)/shard_map/hqk,qhd->khd/dot_general | solution.py:88
  142.6 0.6 slice-done.4
  143.2 0.6 slice-done.5
  143.9 0.5 copy-done.3
  144.3 5.0 %multiply_reduce_fusion = (f32[3,384]{1,0:T(4,128)S(1)}, f32[3,384,2304]{1,2,0:T(8,128)}) fusion(f32[3,384,2304]{1,2,0:T(8,128)S(1)} %bitcast.85, f32[3,384]{1,0:T(4,128)S(1)} %get-tuple-element.19, bf16[384,3,128]{0,2,1:T(8,128)(2,1)S(1)} %bitcast.109, bf16[2304,3,128]{0,2,1:T(8,128)(2,1)S(1)} %bitcast.90), kind=kOutput, calls=%fused_computation.11 | convolution fusion | flops 687438720 | bytes 23307264 | tf_op jit(solution)/shard_map/qhd,khd->hqk/dot_general | solution.py:71
  149.4 8.3 %multiply_convert_fusion = bf16[3,384,2304]{1,2,0:T(8,128)(2,1)S(1)} fusion(f32[3,384,2304]{1,2,0:T(8,128)} %get-tuple-element.22, f32[3,384]{1,0:T(4,128)S(1)} %get-tuple-element.21, f32[3,384,2304]{1,2,0:T(8,128)} %get-tuple-element.20, f32[3,384]{1,0:T(4,128)S(1)} %get-tuple-element.19), kind=kLoop, calls=%fused_computation.10 | loop fusion | flops 10616832 | bytes 26551296 | tf_op jit(solution)/shard_map/convert_element_type | solution.py:75
  157.7 1.9 fusion.29
  159.5 3.4 %fusion.21 = f32[2304,3,128]{0,2,1:T(8,128)} fusion(bf16[3,384,2304]{1,2,0:T(8,128)(2,1)S(1)} %multiply_convert_fusion, bf16[384,3,128]{0,2,1:T(8,128)(2,1)S(1)} %bitcast.96), kind=kOutput, calls=%fused_computation.31 | convolution fusion | flops 680361984 | bytes 9142272 | tf_op jit(solution)/shard_map/hqk,qhd->khd/dot_general | solution.py:84
  162.9 1.6 fusion.22
  164.5 5.0 %multiply_reduce_fusion.1 = (f32[3,384]{1,0:T(4,128)S(1)}, f32[3,384,2304]{1,2,0:T(8,128)}) fusion(f32[3,384,2304]{1,2,0:T(8,128)S(1)} %bitcast.83, f32[3,384]{1,0:T(4,128)S(1)} %get-tuple-element.23, bf16[384,3,128]{0,2,1:T(8,128)(2,1)S(1)} %bitcast.107, bf16[2304,3,128]{0,2,1:T(8,128)(2,1)S(1)} %bitcast.91), kind=kOutput, calls=%fused_computation.14 | convolution fusion | flops 687438720 | bytes 23307264 | tf_op jit(solution)/shard_map/qhd,khd->hqk/dot_general | solution.py:71
  169.5 1.2 fusion.41
  170.7 1.9 copy.74
  172.6 1.8 copy.77
  174.4 1.8 copy.76
  176.3 0.9 copy.75
  177.2 2.0 pad_maximum_fusion.5
  179.2 1.3 collective-permute-start.6
  180.5 1.9 pad_maximum_fusion.6
  182.4 5.4 %collective-permute-start.7 = (bf16[768,384]{1,0:T(8,128)(2,1)}, bf16[768,384]{1,0:T(8,128)(2,1)}, u32[]{:S(2)}, u32[]{:S(2)}) collective-permute-start(bf16[768,384]{1,0:T(8,128)(2,1)} %pad_maximum_fusion.6), channel_id=1, source_target_pairs={{0,4},{4,8},{8,12},{12,16},{16,20},{20,24},{24,28},{1,5},{5,9},{9,... | collective-permute-start | bytes 1769480 | tf_op jit(solution)/shard_map/ppermute | solution.py:17
  187.7 7.9 %multiply_convert_fusion.1 = bf16[3,384,2304]{1,2,0:T(8,128)(2,1)S(1)} fusion(f32[3,384,2304]{1,2,0:T(8,128)} %get-tuple-element.26, f32[3,384]{1,0:T(4,128)S(1)} %get-tuple-element.25, f32[3,384,2304]{1,2,0:T(8,128)} %get-tuple-element.24, f32[3,384]{1,0:T(4,128)S(1)} %get-tuple-element.23), kind=kLoop, calls=%fused_computation.13 | loop fusion | flops 10616832 | bytes 26551296 | tf_op jit(solution)/shard_map/convert_element_type | solution.py:75
  195.7 1.6 fusion.20
  197.3 1.1 copy-done
  198.4 1.2 copy-done.1
  199.6 1.4 fusion.45
  201.0 1.9 copy.66
  202.8 1.9 copy.69
  204.7 1.9 copy.68
  206.5 1.8 copy.67
  208.4 1.9 pad_maximum_fusion.3
  210.3 1.3 collective-permute-start.4
  211.6 1.9 pad_maximum_fusion.4
  213.5 5.4 %collective-permute-start.5 = (bf16[768,384]{1,0:T(8,128)(2,1)}, bf16[768,384]{1,0:T(8,128)(2,1)}, u32[]{:S(2)}, u32[]{:S(2)}) collective-permute-start(bf16[768,384]{1,0:T(8,128)(2,1)} %pad_maximum_fusion.4), channel_id=1, source_target_pairs={{0,4},{4,8},{8,12},{12,16},{16,20},{20,24},{24,28},{1,5},{5,9},{9,... | collective-permute-start | bytes 1769480 | tf_op jit(solution)/shard_map/ppermute | solution.py:17
  218.9 4.3 %fusion.28 = bf16[3,128,384]{2,1,0:T(8,128)(2,1)} fusion(bf16[2304,3,128]{0,2,1:T(8,128)(2,1)S(1)} %bitcast.81, bf16[3,384,2304]{1,2,0:T(8,128)(2,1)} %copy-done), kind=kOutput, calls=%fused_computation.39 | convolution fusion | flops 679772160 | bytes 7372800 | tf_op jit(solution)/shard_map/hqk,khd->qhd/dot_general | solution.py:78
  223.2 1.9 copy.61
  225.1 0.2 copy.73
  225.4 0.2 copy.72
  225.6 1.2 copy.60
  226.8 0.2 copy.65
  227.0 0.2 copy.64
  227.3 1.8 pad_maximum_fusion.2
  229.1 2.2 fusion.33
  231.4 8.7 %collective-permute-done.5 = bf16[768,384]{1,0:T(8,128)(2,1)} collective-permute-done((bf16[768,384]{1,0:T(8,128)(2,1)}, bf16[768,384]{1,0:T(8,128)(2,1)}, u32[]{:S(2)}, u32[]{:S(2)}) %collective-permute-start.5) | collective-permute-done | bytes 589856 | tf_op jit(solution)/shard_map/ppermute | solution.py:17
  240.0 2.2 fusion.31
  (32 shorter events, 0.3 us)
Async XLA Ops:
  7.2 18.5 %copy-start.5 = (bf16[768,384]{1,0:T(8,128)(2,1)S(1)}, bf16[768,384]{1,0:T(8,128)(2,1)}, u32[]{:S(2)}) copy-start(bf16[768,384]{1,0:T(8,128)(2,1)} %param.5) | copy-start | bytes 1769476
  7.2 85.3 %all-gather.5.cloned.1.call-start = ((), (), s32[]{:S(2)}) async-start(), calls=%async_computation.1 | async-start | bytes 2654208 | tf_op jit(solution)/shard_map/all_gather | solution.py:36
  7.9 123.7 %all-gather.3.cloned.1.call-start = ((), (), s32[]{:S(2)}) async-start(), calls=%async_computation | async-start | bytes 5898240 | tf_op jit(solution)/shard_map/all_gather | solution.py:32
  10.0 22.2 %collective-permute-start.3 = (bf16[768,384]{0,1:T(8,128)(2,1)S(1)}, bf16[768,384]{0,1:T(8,128)(2,1)S(1)}, u32[]{:S(2)}, u32[]{:S(2)}) collective-permute-start(bf16[768,384]{0,1:T(8,128)(2,1)S(1)} %copy.44), channel_id=1, source_target_pairs={{4,0},{8,4},{12,8},{16,12},{20,16},{24,20},{28,24},{5,1},{9,5},{13... | collective-permute-start | bytes 1769480 | tf_op jit(solution)/shard_map/ppermute | solution.py:17
  11.3 45.6 %collective-permute-start.2 = (bf16[768,384]{0,1:T(8,128)(2,1)S(1)}, bf16[768,384]{0,1:T(8,128)(2,1)}, u32[]{:S(2)}, u32[]{:S(2)}) collective-permute-start(bf16[768,384]{0,1:T(8,128)(2,1)S(1)} %copy.44), channel_id=1, source_target_pairs={{0,4},{4,8},{8,12},{12,16},{16,20},{20,24},{24,28},{1,5},{5,9},{9,... | collective-permute-start | bytes 1769480 | tf_op jit(solution)/shard_map/ppermute | solution.py:17
  18.9 40.4 %collective-permute-start.1 = (bf16[768,384]{0,1:T(8,128)(2,1)S(1)}, bf16[768,384]{0,1:T(8,128)(2,1)S(1)}, u32[]{:S(2)}, u32[]{:S(2)}) collective-permute-start(bf16[768,384]{0,1:T(8,128)(2,1)S(1)} %copy.38), channel_id=1, source_target_pairs={{4,0},{8,4},{12,8},{16,12},{20,16},{24,20},{28,24},{5,1},{9,5},{13... | collective-permute-start | bytes 1769480 | tf_op jit(solution)/shard_map/ppermute | solution.py:17
  20.2 51.8 %collective-permute-start = (bf16[768,384]{0,1:T(8,128)(2,1)S(1)}, bf16[768,384]{0,1:T(8,128)(2,1)}, u32[]{:S(2)}, u32[]{:S(2)}) collective-permute-start(bf16[768,384]{0,1:T(8,128)(2,1)S(1)} %copy.38), channel_id=1, source_target_pairs={{0,4},{4,8},{8,12},{12,16},{16,20},{20,24},{24,28},{1,5},{5,9},{9,... | collective-permute-start | bytes 1769480 | tf_op jit(solution)/shard_map/ppermute | solution.py:17
  59.4 0.8 copy-start.4
  136.7 5.9 %slice-start.3 = ((s8[10616832]{0:T(1024)(128)(4,1)}), s8[4194304]{0:T(1024)(128)(4,1)S(1)}, s32[]{:S(2)}) async-start(s8[10616832]{0:T(1024)(128)(4,1)} %bitcast.84), calls=%async_computation.5 | async-start | bytes 8388608
  136.8 6.4 %slice-start.4 = ((s8[10616832]{0:T(1024)(128)(4,1)}), s8[4194304]{0:T(1024)(128)(4,1)S(1)}, s32[]{:S(2)}) async-start(s8[10616832]{0:T(1024)(128)(4,1)} %bitcast.84), calls=%async_computation.6 | async-start | bytes 8388608
  136.8 7.1 %slice-start.5 = ((s8[10616832]{0:T(1024)(128)(4,1)}), s8[2228224]{0:T(1024)(128)(4,1)S(1)}, s32[]{:S(2)}) async-start(s8[10616832]{0:T(1024)(128)(4,1)} %bitcast.84), calls=%async_computation.7 | async-start | bytes 4456448
  136.8 7.5 %copy-start.3 = (bf16[2304,384]{0,1:T(8,128)(2,1)S(1)}, bf16[2304,384]{0,1:T(8,128)(2,1)}, u32[]{:S(2)}) copy-start(bf16[2304,384]{0,1:T(8,128)(2,1)} %pad_maximum_fusion.1) | copy-start | bytes 5308420
  149.4 13.5 %slice-start = ((s8[10616832]{0:T(1024)(128)(4,1)}), s8[4194304]{0:T(1024)(128)(4,1)S(1)}, s32[]{:S(2)}) async-start(s8[10616832]{0:T(1024)(128)(4,1)} %bitcast.82), calls=%async_computation.2 | async-start | bytes 8388608
  149.4 13.5 %slice-start.1 = ((s8[10616832]{0:T(1024)(128)(4,1)}), s8[4194304]{0:T(1024)(128)(4,1)S(1)}, s32[]{:S(2)}) async-start(s8[10616832]{0:T(1024)(128)(4,1)} %bitcast.82), calls=%async_computation.3 | async-start | bytes 8388608
  157.7 5.2 %slice-start.2 = ((s8[10616832]{0:T(1024)(128)(4,1)}), s8[2228224]{0:T(1024)(128)(4,1)S(1)}, s32[]{:S(2)}) async-start(s8[10616832]{0:T(1024)(128)(4,1)} %bitcast.82), calls=%async_computation.4 | async-start | bytes 4456448
  179.2 49.9 %collective-permute-start.6 = (bf16[768,384]{1,0:T(8,128)(2,1)}, bf16[768,384]{1,0:T(8,128)(2,1)}, u32[]{:S(2)}, u32[]{:S(2)}) collective-permute-start(bf16[768,384]{1,0:T(8,128)(2,1)} %pad_maximum_fusion.5), channel_id=1, source_target_pairs={{4,0},{8,4},{12,8},{16,12},{20,16},{24,20},{28,24},{5,1},{9,5},{13... | collective-permute-start | bytes 1769480 | tf_op jit(solution)/shard_map/ppermute | solution.py:17
  182.4 46.7 %collective-permute-start.7 = (bf16[768,384]{1,0:T(8,128)(2,1)}, bf16[768,384]{1,0:T(8,128)(2,1)}, u32[]{:S(2)}, u32[]{:S(2)}) collective-permute-start(bf16[768,384]{1,0:T(8,128)(2,1)} %pad_maximum_fusion.6), channel_id=1, source_target_pairs={{0,4},{4,8},{8,12},{12,16},{16,20},{20,24},{24,28},{1,5},{5,9},{9,... | collective-permute-start | bytes 1769480 | tf_op jit(solution)/shard_map/ppermute | solution.py:17
  195.7 2.7 %copy-start = (bf16[3,384,2304]{1,2,0:T(8,128)(2,1)}, bf16[3,384,2304]{1,2,0:T(8,128)(2,1)S(1)}, u32[]{:S(2)}) copy-start(bf16[3,384,2304]{1,2,0:T(8,128)(2,1)S(1)} %multiply_convert_fusion.1) | copy-start | bytes 15925252
  195.7 3.9 %copy-start.1 = (f32[2304,3,128]{0,2,1:T(8,128)S(1)}, f32[2304,3,128]{0,2,1:T(8,128)}, u32[]{:S(2)}) copy-start(f32[2304,3,128]{0,2,1:T(8,128)} %fusion.21) | copy-start | bytes 10616836
  210.3 21.0 %collective-permute-start.4 = (bf16[768,384]{1,0:T(8,128)(2,1)}, bf16[768,384]{1,0:T(8,128)(2,1)}, u32[]{:S(2)}, u32[]{:S(2)}) collective-permute-start(bf16[768,384]{1,0:T(8,128)(2,1)} %pad_maximum_fusion.3), channel_id=1, source_target_pairs={{4,0},{8,4},{12,8},{16,12},{20,16},{24,20},{28,24},{5,1},{9,5},{13... | collective-permute-start | bytes 1769480 | tf_op jit(solution)/shard_map/ppermute | solution.py:17
  213.5 26.5 %collective-permute-start.5 = (bf16[768,384]{1,0:T(8,128)(2,1)}, bf16[768,384]{1,0:T(8,128)(2,1)}, u32[]{:S(2)}, u32[]{:S(2)}) collective-permute-start(bf16[768,384]{1,0:T(8,128)(2,1)} %pad_maximum_fusion.4), channel_id=1, source_target_pairs={{0,4},{4,8},{8,12},{12,16},{16,20},{20,24},{24,28},{1,5},{5,9},{9,... | collective-permute-start | bytes 1769480 | tf_op jit(solution)/shard_map/ppermute | solution.py:17
  223.2 3.6 %copy-start.2 = (f32[384,3,128]{0,2,1:T(8,128)S(1)}, f32[384,3,128]{0,2,1:T(8,128)}, u32[]{:S(2)}) copy-start(f32[384,3,128]{0,2,1:T(8,128)} %get-tuple-element.13) | copy-start | bytes 1769476
Sparse Core Ops, SparseCore 0:
  10.0 82.4 all-gather.4
  94.1 37.4 all-gather.2
where the time goes:
time: 250 us; the launch traced here: 249 us
  waiting for transfers between devices  95.2 us (38%)
  matrix products  49.2 us (20%)
  other arithmetic  36.7 us (15%)
  starting transfers between devices  27.8 us (11%)
  local copies, waits for them, and re-layouts  25.9 us (10%)
  between operations  14.3 us (6%)
    ppermute x8, waiting for transfers between devices, passed_along(): return lax.ppermute(block, axis, route)  51.1 us
    all_gather x1, waiting for transfers between devices, local(): full_grad = lax.all_gather(grad_out, 'head', axis=1, tiled=True)  39.1 us
    ppermute x8, starting transfers between devices, passed_along(): return lax.ppermute(block, axis, route)  27.7 us
    convert_element_type x2, other arithmetic, local(): (softmax_rows * (softmax_grad - row_inner)).astype(jnp.bfloat16)  16.2 us
    sub x2, matrix products, local(): weights = jnp.exp(scores - row_peak)  15.5 us
    dot_general x2, matrix products, local(): jnp.einsum('qhd,khd->hqk', grad_tile, value_block, preferred_element_type...  9.98 us
    add x6, local copies, waits for them, and re-layouts, local(): key_sums[slab_index][neighbour] + key_part[offset:offset + tile_size]  7.88 us
    unnamed x28, local copies, waits for them, and re-layouts  7.88 us
  transfers between devices with their start and end apart: 10, of which 6 were waited for; matrix products, arithmetic and copies ran while one was open for 24% of the time, Pallas kernels for 0%

commit v1 on v0

--- a/solution.py
+++ b/solution.py
@@ -9,6 +9,18 @@
 TILE_H = 8
 TILE_W = 8
 VT = 8
+
+
+def gather_by_bits(x, axis, dim):
+    ways, here, lap = (lax.axis_size(axis), lax.axis_index(axis), x.shape[dim])
+    line, have = (x, 1)
+    while have < ways:
+        line = jnp.concatenate(
+            [line, lax.ppermute(line, axis, [(d, (d - have) % ways) for d in range(ways)])],
+            axis=dim,
+        )
+        have = 2 * have
+    return jnp.roll(line, here * lap, axis=dim)
 
 
 def passed_along(block, axis, distance):
@@ -29,7 +41,7 @@
     inverse_root = 1.0 / math.sqrt(HD)
     video_place = lax.axis_index("tm") % VT
     flags = (video_place > 0, video_place >= 0, video_place < VT - 1)
-    full_grad = lax.all_gather(grad_out, "head", axis=1, tiled=True)
+    full_grad = gather_by_bits(grad_out, "head", 1)
     attn_sum = jnp.einsum(
         "td,hd->th",
         full_grad,

time: 250 us -> 221 us (0.88)
  waiting for transfers between devices: 95.2 us -> 41.4 us
  local copies, waits for them, and re-layouts: 25.9 us -> 42.9 us
  matrix products: 49.2 us -> 53 us
  starting transfers between devices: 27.8 us -> 31.2 us
    all_gather x1 -> x0, waiting for transfers between devices: 39.1 us -> none  [local(): full_grad = lax.all_gather(grad_out, 'head', axis=1, tiled=True)]
    unnamed x28 -> x45, local copies, waits for them, and re-layouts: 7.88 us -> 18.9 us
    ppermute x8, waiting for transfers between devices: 51.1 us -> 41.4 us  [passed_along(): return lax.ppermute(block, axis, route)]
    all_gather x1, waiting for transfers between devices: 3.64 us -> 0.01 us  [local(): lax.all_gather(w_out, 'tm', axis=1, tiled=True)]
    ppermute x0 -> x2, starting transfers between devices: none -> 3.63 us  [gather_by_bits(): lax.ppermute(line, axis, [(d, (d - have) % ways) for d in range(ways)])]
    concatenate x0 -> x1, local copies, waits for them, and re-layouts: none -> 3.25 us  [gather_by_bits(): return jnp.roll(line, here * lap, axis=dim)]
  transfers between devices with their start and end apart: 10 -> 11, of which waited for: 6 -> 3; matrix products, arithmetic and copies ran while one was open for 24% -> 37% of each run, Pallas kernels for 0% -> 0%
where the time goes in v1:
time: 221 us; the launch traced here: 219 us
  matrix products  53 us (24%)
  local copies, waits for them, and re-layouts  42.9 us (19%)
  waiting for transfers between devices  41.4 us (19%)
  other arithmetic  36.7 us (17%)
  starting transfers between devices  31.2 us (14%)
  between operations  14.3 us (6%)
    ppermute x8, waiting for transfers between devices, passed_along(): return lax.ppermute(block, axis, route)  41.4 us
    ppermute x8, starting transfers between devices, passed_along(): return lax.ppermute(block, axis, route)  27.5 us
    unnamed x45, local copies, waits for them, and re-layouts  18.9 us
    sub x2, matrix products, local(): weights = jnp.exp(scores - row_peak)  17.2 us
    convert_element_type x2, other arithmetic, local(): (softmax_rows * (softmax_grad - row_inner)).astype(jnp.bfloat16)  14.2 us
    dot_general x2, matrix products, local(): jnp.einsum('qhd,khd->hqk', grad_tile, value_block, preferred_element_type...  9.92 us
    dot_general x2, matrix products, local(): jnp.einsum('hqk,qhd->khd', softmax_low, grad_tile, preferred_element_type...  9.25 us
    add x6, local copies, waits for them, and re-layouts, local(): key_sums[slab_index][neighbour] + key_part[offset:offset + tile_size]  7.88 us
  transfers between devices with their start and end apart: 11, of which 3 were waited for; matrix products, arithmetic and copies ran while one was open for 37% of the time, Pallas kernels for 0%

profile of v1, /device:TPU:0, one launch (start us, length us, event | category | flops | bytes accessed | tf_op | source)
XLA Modules:
  0.0 219.5 jit_solution(13571025478446271425)
XLA Ops:
  7.2 2.5 %collective-permute-start.2 = (bf16[768,768]{1,0:T(8,128)(2,1)}, bf16[768,768]{1,0:T(8,128)(2,1)S(1)}, u32[]{:S(2)}, u32[]{:S(2)}) collective-permute-start(bf16[768,768]{1,0:T(8,128)(2,1)} %param.8), channel_id=1, source_target_pairs={{0,3},{1,0},{2,1},{3,2},{4,7},{5,4},{6,5},{7,6},{8,11},{9,8},{10,9... | collective-permute-start | bytes 3538952 | tf_op jit(solution)/shard_map/ppermute | solution.py:19
  9.7 1.3 copy.44
  11.0 1.3 collective-permute-start.5
  12.3 5.4 %collective-permute-start.4 = (bf16[768,384]{0,1:T(8,128)(2,1)S(1)}, bf16[768,384]{0,1:T(8,128)(2,1)}, u32[]{:S(2)}, u32[]{:S(2)}) collective-permute-start(bf16[768,384]{0,1:T(8,128)(2,1)S(1)} %copy.44), channel_id=1, source_target_pairs={{0,4},{4,8},{8,12},{12,16},{16,20},{20,24},{24,28},{1,5},{5,9},{9,... | collective-permute-start | bytes 1769480 | tf_op jit(solution)/shard_map/ppermute | solution.py:29
  17.7 1.3 copy.38
  19.0 1.3 collective-permute-start.1
  20.3 5.4 %collective-permute-start = (bf16[768,384]{0,1:T(8,128)(2,1)S(1)}, bf16[768,384]{0,1:T(8,128)(2,1)}, u32[]{:S(2)}, u32[]{:S(2)}) collective-permute-start(bf16[768,384]{0,1:T(8,128)(2,1)S(1)} %copy.38), channel_id=1, source_target_pairs={{0,4},{4,8},{8,12},{12,16},{16,20},{20,24},{24,28},{1,5},{5,9},{9,... | collective-permute-start | bytes 1769480 | tf_op jit(solution)/shard_map/ppermute | solution.py:29
  25.7 1.9 fusion.56
  27.6 1.8 pad_maximum_fusion
  29.4 1.2 collective-permute-start.3
  30.6 1.9 copy.94
  32.5 1.8 copy.95
  34.3 1.1 constant_dynamic-update-slice_fusion.5
  35.4 20.7 %collective-permute-done.4 = bf16[768,384]{0,1:T(8,128)(2,1)} collective-permute-done((bf16[768,384]{0,1:T(8,128)(2,1)S(1)}, bf16[768,384]{0,1:T(8,128)(2,1)}, u32[]{:S(2)}, u32[]{:S(2)}) %collective-permute-start.4) | collective-permute-done | bytes 589856 | tf_op jit(solution)/shard_map/ppermute | solution.py:29
  56.2 2.6 %pad_maximum_fusion.2 = bf16[2304,384]{0,1:T(8,128)(2,1)} fusion(bf16[768,384]{0,1:T(8,128)(2,1)} %collective-permute-done.5, bf16[768,384]{0,1:T(8,128)(2,1)S(1)} %copy.44, bf16[768,384]{0,1:T(8,128)(2,1)} %collective-permute-done.4), kind=kLoop, calls=%fused_computation.38 | loop fusion | flops 5308416 | bytes 3538944 | tf_op jit(solution)/shard_map/concatenate | solution.py:65
  58.7 12.6 %collective-permute-done = bf16[768,384]{0,1:T(8,128)(2,1)} collective-permute-done((bf16[768,384]{0,1:T(8,128)(2,1)S(1)}, bf16[768,384]{0,1:T(8,128)(2,1)}, u32[]{:S(2)}, u32[]{:S(2)}) %collective-permute-start) | collective-permute-done | bytes 589856 | tf_op jit(solution)/shard_map/ppermute | solution.py:29
  71.3 1.4 pad_maximum_fusion.1
  72.7 8.7 %fusion.58 = (f32[3,384]{1,0:T(4,128)S(1)}, f32[3,384,2304]{1,2,0:T(8,128)}) fusion(pred[2304]{0:T(1024)(128)(4,1)S(1)} %pad_add_fusion, bf16[2304,3,128]{0,2,1:T(8,128)(2,1)S(1)} %bitcast.77, bf16[384,3,128]{0,2,1:T(8,128)(2,1)} %bitcast.94), kind=kOutput, calls=%fused_computation.91 | convolution fusion | flops 690096384 | bytes 12688128 | tf_op jit(solution)/shard_map/sub | solution.py:80
  81.4 8.5 %fusion.59 = (f32[3,384]{1,0:T(4,128)S(1)}, f32[3,384,2304]{1,2,0:T(8,128)}) fusion(pred[2304]{0:T(1024)(128)(4,1)} %copy-done.11, bf16[2304,3,128]{0,2,1:T(8,128)(2,1)S(1)} %bitcast.78, bf16[384,3,128]{0,2,1:T(8,128)(2,1)S(1)} %bitcast.91), kind=kOutput, calls=%fused_computation.92 | convolution fusion | flops 690096384 | bytes 12688128 | tf_op jit(solution)/shard_map/sub | solution.py:80
  89.9 2.4 %constant_dynamic-update-slice_fusion.4 = bf16[768,6144]{1,0:T(8,128)(2,1)} fusion(bf16[768,6144]{1,0:T(8,128)(2,1)} %constant_dynamic-update-slice_fusion.5, bf16[768,768]{1,0:T(8,128)(2,1)} %copy-done.3), kind=kLoop, calls=%fused_computation.81 | loop fusion | bytes 2359296
  92.3 3.4 %constant_dynamic-update-slice_fusion.3 = bf16[768,6144]{1,0:T(8,128)(2,1)} fusion(bf16[768,6144]{1,0:T(8,128)(2,1)} %constant_dynamic-update-slice_fusion.4, bf16[768,1536]{1,0:T(8,128)(2,1)} %collective-permute-done.3), kind=kLoop, calls=%fused_computation.80 | loop fusion | bytes 4718592
  95.8 1.1 constant_dynamic-update-slice_fusion.2
  96.9 1.2 constant_dynamic-update-slice_fusion.1
  98.1 3.2 %constant_dynamic-update-slice_fusion = bf16[768,6144]{1,0:T(8,128)(2,1)} fusion(bf16[768,6144]{1,0:T(8,128)(2,1)} %constant_dynamic-update-slice_fusion.1, bf16[768,1536]{1,0:T(8,128)(2,1)} %collective-permute-done.3), kind=kLoop, calls=%fused_computation.77 | loop fusion | bytes 4718592 | tf_op jit(solution)/shard_map/jit(_roll_dynamic)/concatenate | solution.py:23
  101.3 5.5 %fusion.30 = bf16[768,384]{0,1:T(8,128)(2,1)S(1)} fusion(bf16[384,3072]{1,0:T(8,128)(2,1)} %all-gather.2.cloned.1.call-done, bf16[768,6144]{1,0:T(8,128)(2,1)} %constant_dynamic-update-slice_fusion, s32[]{:T(128)S(6)} %select_n.36), kind=kOutput, calls=%fused_computation.39 | convolution fusion | flops 1812234240 | bytes 7667716 | tf_op jit(solution)/shard_map/td,hd->th/dot_general | solution.py:45
  106.8 0.2 fusion.57
  107.1 7.6 %fusion.27 = f32[2304,3,128]{0,2,1:T(8,128)} fusion(bf16[384,3,128]{0,2,1:T(8,128)(2,1)S(1)} %bitcast.107, f32[3,384,2304]{1,2,0:T(8,128)} %get-tuple-element.20, f32[3,384]{1,0:T(4,128)S(1)} %get-tuple-element.19), kind=kOutput, calls=%fused_computation.35 | convolution fusion | flops 684785664 | bytes 14455296 | tf_op jit(solution)/shard_map/hqk,qhd->khd/dot_general | solution.py:100
  114.8 1.0 copy-done.7
  115.8 4.9 %multiply_reduce_fusion = (f32[3,384]{1,0:T(4,128)S(1)}, f32[3,384,2304]{1,2,0:T(8,128)}) fusion(f32[3,384,2304]{1,2,0:T(8,128)S(1)} %bitcast.84, f32[3,384]{1,0:T(4,128)S(1)} %get-tuple-element.19, bf16[384,3,128]{0,2,1:T(8,128)(2,1)S(1)} %bitcast.108, bf16[2304,3,128]{0,2,1:T(8,128)(2,1)S(1)} %bitcast.89), kind=kOutput, calls=%fused_computation.11 | convolution fusion | flops 687438720 | bytes 23307264 | tf_op jit(solution)/shard_map/qhd,khd->hqk/dot_general | solution.py:83
  120.7 6.3 %multiply_convert_fusion = bf16[3,384,2304]{1,2,0:T(8,128)(2,1)S(1)} fusion(f32[3,384,2304]{1,2,0:T(8,128)} %get-tuple-element.22, f32[3,384]{1,0:T(4,128)S(1)} %get-tuple-element.21, f32[3,384,2304]{1,2,0:T(8,128)S(1)} %bitcast.84, f32[3,384]{1,0:T(4,128)S(1)} %get-tuple-element.19), kind=kLoop, calls=%fused_computation.10 | loop fusion | flops 10616832 | bytes 26551296 | tf_op jit(solution)/shard_map/convert_element_type | solution.py:87
  127.0 1.8 fusion.34
  128.9 3.4 %fusion.23 = f32[2304,3,128]{0,2,1:T(8,128)} fusion(bf16[3,384,2304]{1,2,0:T(8,128)(2,1)S(1)} %multiply_convert_fusion, bf16[384,3,128]{0,2,1:T(8,128)(2,1)S(1)} %bitcast.95), kind=kOutput, calls=%fused_computation.33 | convolution fusion | flops 680361984 | bytes 9142272 | tf_op jit(solution)/shard_map/hqk,qhd->khd/dot_general | solution.py:96
  132.3 1.6 fusion.24
  133.9 5.0 %multiply_reduce_fusion.1 = (f32[3,384]{1,0:T(4,128)S(1)}, f32[3,384,2304]{1,2,0:T(8,128)}) fusion(f32[3,384,2304]{1,2,0:T(8,128)S(1)} %bitcast.82, f32[3,384]{1,0:T(4,128)S(1)} %get-tuple-element.23, bf16[384,3,128]{0,2,1:T(8,128)(2,1)S(1)} %bitcast.106, bf16[2304,3,128]{0,2,1:T(8,128)(2,1)S(1)} %bitcast.90), kind=kOutput, calls=%fused_computation.14 | convolution fusion | flops 687438720 | bytes 23307264 | tf_op jit(solution)/shard_map/qhd,khd->hqk/dot_general | solution.py:83
  138.9 1.2 fusion.46
  140.1 1.9 copy.74
  142.0 1.8 copy.77
  143.8 1.8 copy.76
  145.7 0.9 copy.75
  146.5 2.0 pad_maximum_fusion.6
  148.5 1.3 collective-permute-start.8
  149.8 1.9 pad_maximum_fusion.7
  151.8 5.9 %collective-permute-start.9 = (bf16[768,384]{1,0:T(8,128)(2,1)}, bf16[768,384]{1,0:T(8,128)(2,1)}, u32[]{:S(2)}, u32[]{:S(2)}) collective-permute-start(bf16[768,384]{1,0:T(8,128)(2,1)} %pad_maximum_fusion.7), channel_id=1, source_target_pairs={{0,4},{4,8},{8,12},{12,16},{16,20},{20,24},{24,28},{1,5},{5,9},{9,... | collective-permute-start | bytes 1769480 | tf_op jit(solution)/shard_map/ppermute | solution.py:29
  157.7 8.0 %multiply_convert_fusion.1 = bf16[3,384,2304]{1,2,0:T(8,128)(2,1)S(1)} fusion(f32[3,384,2304]{1,2,0:T(8,128)} %get-tuple-element.26, f32[3,384]{1,0:T(4,128)S(1)} %get-tuple-element.25, f32[3,384,2304]{1,2,0:T(8,128)} %get-tuple-element.24, f32[3,384]{1,0:T(4,128)S(1)} %get-tuple-element.23), kind=kLoop, calls=%fused_computation.13 | loop fusion | flops 10616832 | bytes 26551296 | tf_op jit(solution)/shard_map/convert_element_type | solution.py:87
  165.7 1.6 fusion.22
  167.3 1.1 copy-done
  168.4 1.2 copy-done.1
  169.6 1.4 fusion.50
  171.0 1.9 copy.66
  172.8 1.9 copy.69
  174.7 1.9 copy.68
  176.5 1.8 copy.67
  178.4 1.9 pad_maximum_fusion.4
  180.3 1.3 collective-permute-start.6
  181.6 1.9 pad_maximum_fusion.5
  183.5 5.7 %collective-permute-start.7 = (bf16[768,384]{1,0:T(8,128)(2,1)}, bf16[768,384]{1,0:T(8,128)(2,1)}, u32[]{:S(2)}, u32[]{:S(2)}) collective-permute-start(bf16[768,384]{1,0:T(8,128)(2,1)} %pad_maximum_fusion.5), channel_id=1, source_target_pairs={{0,4},{4,8},{8,12},{12,16},{16,20},{20,24},{24,28},{1,5},{5,9},{9,... | collective-permute-start | bytes 1769480 | tf_op jit(solution)/shard_map/ppermute | solution.py:29
  189.2 4.3 %fusion.33 = bf16[3,128,384]{2,1,0:T(8,128)(2,1)} fusion(bf16[2304,3,128]{0,2,1:T(8,128)(2,1)S(1)} %bitcast.80, bf16[3,384,2304]{1,2,0:T(8,128)(2,1)} %copy-done), kind=kOutput, calls=%fused_computation.42 | convolution fusion | flops 679772160 | bytes 7372800 | tf_op jit(solution)/shard_map/hqk,khd->qhd/dot_general | solution.py:90
  193.5 1.9 copy.61
  195.6 0.2 copy.72
  195.9 1.9 copy.60
  198.2 1.9 pad_maximum_fusion.3
  200.1 2.2 %fusion.38 = bf16[768,384]{1,0:T(8,128)(2,1)} fusion(f32[384,384]{1,0:T(8,128)S(1)} %copy.73, f32[384,384]{1,0:T(8,128)S(1)} %copy.72, bf16[768,384]{1,0:T(8,128)(2,1)} %collective-permute-done.9, bf16[768,384]{1,0:T(8,128)(2,1)} %collective-permute-done.8), kind=kLoop, calls=%fused_computation.49 | loop fusion | flops 1769472 | bytes 2949120 | tf_op jit(solution)/shard_map/convert_element_type | solution.py:134
  202.4 8.0 %collective-permute-done.7 = bf16[768,384]{1,0:T(8,128)(2,1)} collective-permute-done((bf16[768,384]{1,0:T(8,128)(2,1)}, bf16[768,384]{1,0:T(8,128)(2,1)}, u32[]{:S(2)}, u32[]{:S(2)}) %collective-permute-start.7) | collective-permute-done | bytes 589856 | tf_op jit(solution)/shard_map/ppermute | solution.py:29
  210.4 2.2 %fusion.36 = bf16[768,384]{1,0:T(8,128)(2,1)} fusion(f32[384,384]{1,0:T(8,128)S(1)} %copy.65, f32[384,384]{1,0:T(8,128)S(1)} %copy.64, bf16[768,384]{1,0:T(8,128)(2,1)} %collective-permute-done.7, bf16[768,384]{1,0:T(8,128)(2,1)} %collective-permute-done.6), kind=kLoop, calls=%fused_computation.46 | loop fusion | flops 1769472 | bytes 2949120 | tf_op jit(solution)/shard_map/convert_element_type | solution.py:134
  (52 shorter events, 0.9 us)
Async XLA Ops:
  7.2 20.4 %copy-start.2 = (bf16[768,768]{1,0:T(8,128)(2,1)S(1)}, bf16[768,768]{1,0:T(8,128)(2,1)}, u32[]{:S(2)}) copy-start(bf16[768,768]{1,0:T(8,128)(2,1)} %param.8) | copy-start | bytes 3538948
  7.2 94.1 %all-gather.2.cloned.1.call-start = ((), (), s32[]{:S(2)}) async-start(), calls=%async_computation | async-start | bytes 2654208 | tf_op jit(solution)/shard_map/all_gather | solution.py:48
  7.2 20.4 %collective-permute-start.2 = (bf16[768,768]{1,0:T(8,128)(2,1)}, bf16[768,768]{1,0:T(8,128)(2,1)S(1)}, u32[]{:S(2)}, u32[]{:S(2)}) collective-permute-start(bf16[768,768]{1,0:T(8,128)(2,1)} %param.8), channel_id=1, source_target_pairs={{0,3},{1,0},{2,1},{3,2},{4,7},{5,4},{6,5},{7,6},{8,11},{9,8},{10,9... | collective-permute-start | bytes 3538952 | tf_op jit(solution)/shard_map/ppermute | solution.py:19
  11.0 24.4 %collective-permute-start.5 = (bf16[768,384]{0,1:T(8,128)(2,1)S(1)}, bf16[768,384]{0,1:T(8,128)(2,1)}, u32[]{:S(2)}, u32[]{:S(2)}) collective-permute-start(bf16[768,384]{0,1:T(8,128)(2,1)S(1)} %copy.44), channel_id=1, source_target_pairs={{4,0},{8,4},{12,8},{16,12},{20,16},{24,20},{28,24},{5,1},{9,5},{13... | collective-permute-start | bytes 1769480 | tf_op jit(solution)/shard_map/ppermute | solution.py:29
  12.3 43.9 %collective-permute-start.4 = (bf16[768,384]{0,1:T(8,128)(2,1)S(1)}, bf16[768,384]{0,1:T(8,128)(2,1)}, u32[]{:S(2)}, u32[]{:S(2)}) collective-permute-start(bf16[768,384]{0,1:T(8,128)(2,1)S(1)} %copy.44), channel_id=1, source_target_pairs={{0,4},{4,8},{8,12},{12,16},{16,20},{20,24},{24,28},{1,5},{5,9},{9,... | collective-permute-start | bytes 1769480 | tf_op jit(solution)/shard_map/ppermute | solution.py:29
  19.0 39.8 %collective-permute-start.1 = (bf16[768,384]{0,1:T(8,128)(2,1)S(1)}, bf16[768,384]{0,1:T(8,128)(2,1)}, u32[]{:S(2)}, u32[]{:S(2)}) collective-permute-start(bf16[768,384]{0,1:T(8,128)(2,1)S(1)} %copy.38), channel_id=1, source_target_pairs={{4,0},{8,4},{12,8},{16,12},{20,16},{24,20},{28,24},{5,1},{9,5},{13... | collective-permute-start | bytes 1769480 | tf_op jit(solution)/shard_map/ppermute | solution.py:29
  20.3 51.0 %collective-permute-start = (bf16[768,384]{0,1:T(8,128)(2,1)S(1)}, bf16[768,384]{0,1:T(8,128)(2,1)}, u32[]{:S(2)}, u32[]{:S(2)}) collective-permute-start(bf16[768,384]{0,1:T(8,128)(2,1)S(1)} %copy.38), channel_id=1, source_target_pairs={{0,4},{4,8},{8,12},{12,16},{16,20},{20,24},{24,28},{1,5},{5,9},{9,... | collective-permute-start | bytes 1769480 | tf_op jit(solution)/shard_map/ppermute | solution.py:29
  27.6 7.8 %copy-start.3 = (bf16[768,768]{1,0:T(8,128)(2,1)}, bf16[768,768]{1,0:T(8,128)(2,1)S(1)}, u32[]{:S(2)}) copy-start(bf16[768,768]{1,0:T(8,128)(2,1)S(1)} %collective-permute-done.2) | copy-start | bytes 3538948
  29.4 63.0 %collective-permute-start.3 = (bf16[768,1536]{1,0:T(8,128)(2,1)}, bf16[768,1536]{1,0:T(8,128)(2,1)}, u32[]{:S(2)}, u32[]{:S(2)}) collective-permute-start(bf16[768,1536]{1,0:T(8,128)(2,1)} %pad_maximum_fusion), channel_id=1, source_target_pairs={{0,2},{1,3},{2,0},{3,1},{4,6},{5,7},{6,4},{7,5},{8,10},{9,11},{10,... | collective-permute-start | bytes 7077896 | tf_op jit(solution)/shard_map/ppermute | solution.py:19
  30.6 42.1 %copy-start.11 = (pred[2304]{0:T(1024)(128)(4,1)}, pred[2304]{0:T(1024)(128)(4,1)S(1)}, u32[]{:S(2)}) copy-start(pred[2304]{0:T(1024)(128)(4,1)S(1)} %pad_add_fusion) | copy-start | bytes 6916
  72.7 8.7 %copy-start.9 = (bf16[384,384]{0,1:T(8,128)(2,1)S(1)}, bf16[384,384]{0,1:T(8,128)(2,1)}, u32[]{:S(2)}) copy-start(bf16[384,384]{0,1:T(8,128)(2,1)} %copy.94) | copy-start | bytes 884740
  92.3 4.6 %copy-start.4 = (bf16[768,768]{1,0:T(8,128)(2,1)S(1)}, bf16[768,768]{1,0:T(8,128)(2,1)}, u32[]{:S(2)}) copy-start(bf16[768,768]{1,0:T(8,128)(2,1)} %copy-done.3) | copy-start | bytes 3538948
  106.8 7.9 %slice-start.3 = ((s8[10616832]{0:T(1024)(128)(4,1)}), s8[4194304]{0:T(1024)(128)(4,1)S(1)}, s32[]{:S(2)}) async-start(s8[10616832]{0:T(1024)(128)(4,1)} %bitcast.83), calls=%async_computation.4 | async-start | bytes 8388608
  107.1 7.7 %slice-start.4 = ((s8[10616832]{0:T(1024)(128)(4,1)}), s8[4194304]{0:T(1024)(128)(4,1)S(1)}, s32[]{:S(2)}) async-start(s8[10616832]{0:T(1024)(128)(4,1)} %bitcast.83), calls=%async_computation.5 | async-start | bytes 8388608
  107.1 7.6 %slice-start.5 = ((s8[10616832]{0:T(1024)(128)(4,1)}), s8[2228224]{0:T(1024)(128)(4,1)S(1)}, s32[]{:S(2)}) async-start(s8[10616832]{0:T(1024)(128)(4,1)} %bitcast.83), calls=%async_computation.6 | async-start | bytes 4456448
  107.1 8.6 %copy-start.7 = (bf16[2304,384]{0,1:T(8,128)(2,1)S(1)}, bf16[2304,384]{0,1:T(8,128)(2,1)}, u32[]{:S(2)}) copy-start(bf16[2304,384]{0,1:T(8,128)(2,1)} %pad_maximum_fusion.2) | copy-start | bytes 5308420
  120.7 11.5 %slice-start = ((s8[10616832]{0:T(1024)(128)(4,1)}), s8[4194304]{0:T(1024)(128)(4,1)S(1)}, s32[]{:S(2)}) async-start(s8[10616832]{0:T(1024)(128)(4,1)} %bitcast.81), calls=%async_computation.1 | async-start | bytes 8388608
  120.7 11.5 %slice-start.1 = ((s8[10616832]{0:T(1024)(128)(4,1)}), s8[4194304]{0:T(1024)(128)(4,1)S(1)}, s32[]{:S(2)}) async-start(s8[10616832]{0:T(1024)(128)(4,1)} %bitcast.81), calls=%async_computation.2 | async-start | bytes 8388608
  127.0 1.9 copy-start.10
  127.0 5.2 %slice-start.2 = ((s8[10616832]{0:T(1024)(128)(4,1)}), s8[2228224]{0:T(1024)(128)(4,1)S(1)}, s32[]{:S(2)}) async-start(s8[10616832]{0:T(1024)(128)(4,1)} %bitcast.81), calls=%async_computation.3 | async-start | bytes 4456448
  132.2 1.6 copy-start.8
  133.9 5.0 %copy-start.5 = (f32[2304,3,128]{0,2,1:T(8,128)S(1)}, f32[2304,3,128]{0,2,1:T(8,128)}, u32[]{:S(2)}) copy-start(f32[2304,3,128]{0,2,1:T(8,128)} %fusion.27) | copy-start | bytes 10616836
  148.5 51.6 %collective-permute-start.8 = (bf16[768,384]{1,0:T(8,128)(2,1)}, bf16[768,384]{1,0:T(8,128)(2,1)}, u32[]{:S(2)}, u32[]{:S(2)}) collective-permute-start(bf16[768,384]{1,0:T(8,128)(2,1)} %pad_maximum_fusion.6), channel_id=1, source_target_pairs={{4,0},{8,4},{12,8},{16,12},{20,16},{24,20},{28,24},{5,1},{9,5},{13... | collective-permute-start | bytes 1769480 | tf_op jit(solution)/shard_map/ppermute | solution.py:29
  151.8 48.4 %collective-permute-start.9 = (bf16[768,384]{1,0:T(8,128)(2,1)}, bf16[768,384]{1,0:T(8,128)(2,1)}, u32[]{:S(2)}, u32[]{:S(2)}) collective-permute-start(bf16[768,384]{1,0:T(8,128)(2,1)} %pad_maximum_fusion.7), channel_id=1, source_target_pairs={{0,4},{4,8},{8,12},{12,16},{16,20},{20,24},{24,28},{1,5},{5,9},{9,... | collective-permute-start | bytes 1769480 | tf_op jit(solution)/shard_map/ppermute | solution.py:29
  165.7 2.7 %copy-start = (bf16[3,384,2304]{1,2,0:T(8,128)(2,1)}, bf16[3,384,2304]{1,2,0:T(8,128)(2,1)S(1)}, u32[]{:S(2)}) copy-start(bf16[3,384,2304]{1,2,0:T(8,128)(2,1)S(1)} %multiply_convert_fusion.1) | copy-start | bytes 15925252
  165.7 3.9 %copy-start.1 = (f32[2304,3,128]{0,2,1:T(8,128)S(1)}, f32[2304,3,128]{0,2,1:T(8,128)}, u32[]{:S(2)}) copy-start(f32[2304,3,128]{0,2,1:T(8,128)} %fusion.23) | copy-start | bytes 10616836
  180.3 22.1 %collective-permute-start.6 = (bf16[768,384]{1,0:T(8,128)(2,1)}, bf16[768,384]{1,0:T(8,128)(2,1)}, u32[]{:S(2)}, u32[]{:S(2)}) collective-permute-start(bf16[768,384]{1,0:T(8,128)(2,1)} %pad_maximum_fusion.4), channel_id=1, source_target_pairs={{4,0},{8,4},{12,8},{16,12},{20,16},{24,20},{28,24},{5,1},{9,5},{13... | collective-permute-start | bytes 1769480 | tf_op jit(solution)/shard_map/ppermute | solution.py:29
  183.5 26.9 %collective-permute-start.7 = (bf16[768,384]{1,0:T(8,128)(2,1)}, bf16[768,384]{1,0:T(8,128)(2,1)}, u32[]{:S(2)}, u32[]{:S(2)}) collective-permute-start(bf16[768,384]{1,0:T(8,128)(2,1)} %pad_maximum_fusion.5), channel_id=1, source_target_pairs={{0,4},{4,8},{8,12},{12,16},{16,20},{20,24},{24,28},{1,5},{5,9},{9,... | collective-permute-start | bytes 1769480 | tf_op jit(solution)/shard_map/ppermute | solution.py:29
  193.5 4.2 %copy-start.6 = (f32[384,3,128]{0,2,1:T(8,128)S(1)}, f32[384,3,128]{0,2,1:T(8,128)}, u32[]{:S(2)}) copy-start(f32[384,3,128]{0,2,1:T(8,128)} %get-tuple-element.13) | copy-start | bytes 1769476
Sparse Core Ops, SparseCore 0:
  10.0 81.7 all-gather.1
